TPU v7x, 32 devices: a whole 2x2x4 slice. The times are simulated.
32 devices in a mesh: cp: 8 (over z, y), tp: 4 (over x, core).
Axes of the slice: x: 2, y: 2, z: 4, core: 2. Of those that a mesh axis runs over, the one named last changes fastest.
Arguments:
- queries: bfloat16 [1024, 8, 16, 128], P('cp', None, 'tp'), may hold values from -64 to 64
- key_heads: bfloat16 [1024, 8, 128], P('cp', 'tp'), may hold values from -6 to 6
- value_heads: bfloat16 [1024, 8, 128], P('cp', 'tp'), may hold values from -6 to 6
- grad_out: bfloat16 [1024, 8, 16, 128], P('cp', None, 'tp'), may hold values from -6 to 6
- doc_starts: int32 [1024], replicated, may hold values from 0 to 1024, as said below
Outputs:
- grad_queries: bfloat16 [1024, 8, 16, 128], P('cp', None, 'tp')
- grad_keys: bfloat16 [1024, 8, 128], P('cp', 'tp')
- grad_values: bfloat16 [1024, 8, 128], P('cp', 'tp')
Inputs may be any that keep to these rules, and one draw needn't show every extreme that they name: doc_starts does not fall and doc_starts[0] = 0; the documents are the nonempty runs from one entry to the next (the last to 1024); each has 1 to 384 tokens, the first has exactly 384; entries after the last document's start equal 1024.
All inputs are finite; a program needn't handle non-finite values.
Results may differ from a plain program's by a relative error of at most 0.011.
Values may be sent and summed in bfloat16 or wider, within the bound.
A program may use at most 64 MiB of HBM per device.

v0:
```python
import jax
import jax.numpy as jnp
from jax import lax
from jax.sharding import PartitionSpec as P

REACH = 3


MASKED_LOGIT = -1e30


def as_sent(value):
    return jax.tree.map(lambda a: a.astype(jnp.bfloat16) if a.dtype == jnp.float32 else a, value)


def shifted(block, axis, distance):
    devices = range(lax.axis_size(axis))
    route = [(i - distance, i) for i in devices if i - distance in devices]
    return lax.ppermute(block, axis, route)


def shifted_2(value, axis, steps):
    count = lax.axis_size(axis)
    pairs = [(source, (source + steps) % count) for source in range(count)]
    return lax.ppermute(value, axis, pairs)


def logits_of(queries, key_blk, scaling):
    return scaling * jnp.einsum(
        "ighc,jgc->ghij", queries, key_blk, preferred_element_type=jnp.float32
    )


def absorb(summary, queries, grad_out, key_blk, value_blk, allowed, scaling):
    row_peak, row_total, carried_sum = summary
    logits = logits_of(queries, key_blk, scaling)
    grad_prob = jnp.einsum(
        "ighc,jgc->ghij", grad_out, value_blk, preferred_element_type=jnp.float32
    )
    new_peak = jnp.maximum(row_peak, jnp.max(jnp.where(allowed, logits, MASKED_LOGIT), axis=-1))
    weights = jnp.where(allowed, jnp.exp(logits - new_peak[..., None]), 0.0)
    fading = jnp.exp(row_peak - new_peak)
    return (
        new_peak,
        row_total * fading + jnp.sum(weights, axis=-1),
        carried_sum * fading + jnp.sum(weights * grad_prob, axis=-1),
    )


def gradients(queries, grad_out, key_blk, value_blk, allowed, log_total, row_delta, scaling):
    logits = logits_of(queries, key_blk, scaling)
    grad_prob = jnp.einsum(
        "ighc,jgc->ghij", grad_out, value_blk, preferred_element_type=jnp.float32
    )
    weights = jnp.where(allowed, jnp.exp(logits - log_total[..., None]), 0.0)
    grad_logit = (weights * (grad_prob - row_delta[..., None])).astype(jnp.bfloat16)
    weights_half = weights.astype(jnp.bfloat16)
    grad_query = scaling * jnp.einsum(
        "ghij,jgc->ighc", grad_logit, key_blk, preferred_element_type=jnp.float32
    )
    grad_key = scaling * jnp.einsum(
        "ghij,ighc->jgc", grad_logit, queries, preferred_element_type=jnp.float32
    )
    grad_value = jnp.einsum(
        "ghij,ighc->jgc", weights_half, grad_out, preferred_element_type=jnp.float32
    )
    return (grad_query, grad_key, grad_value)


def per_device(queries, key_heads, value_heads, grad_out, doc_starts):
    tok_rows = queries.shape[0]
    cp_size = lax.axis_size("cp")
    my_index = lax.axis_index("cp")
    scaling = queries.shape[-1] ** (-0.5)
    offsets = jnp.arange(tok_rows, dtype=jnp.int32)
    distances = jnp.arange(REACH + 1, dtype=jnp.int32)
    owners = (my_index - distances) % cp_size
    place_table = owners[:, None] * tok_rows + offsets[None, :]
    below = doc_starts[None, None, :] <= place_table[:, :, None]
    doc_table = jnp.sum(below, axis=-1, dtype=jnp.int32) - 1
    query_pos = place_table[0]
    query_doc = doc_table[0]

    def mask_for(distance):
        key_pos = lax.dynamic_index_in_dim(place_table, distance, 0, keepdims=False)
        key_doc = lax.dynamic_index_in_dim(doc_table, distance, 0, keepdims=False)
        allowed = (key_doc[None, :] == query_doc[:, None]) & (
            key_pos[None, :] <= query_pos[:, None]
        )
        return allowed[None, None]

    group_k, group_v = (
        lax.all_gather(key_heads, "tp", axis=1, tiled=True),
        lax.all_gather(value_heads, "tp", axis=1, tiled=True),
    )
    stat_shape = (group_k.shape[1], queries.shape[2], tok_rows)
    summary = (
        jnp.full(stat_shape, MASKED_LOGIT, jnp.float32),
        jnp.zeros(stat_shape, jnp.float32),
        jnp.zeros(stat_shape, jnp.float32),
    )
    summary = absorb(summary, queries, grad_out, group_k, group_v, mask_for(0), scaling)
    window_k = jnp.zeros((REACH + 1,) + group_k.shape, jnp.bfloat16)
    window_v = jnp.zeros((REACH + 1,) + group_v.shape, jnp.bfloat16)
    window_k = lax.dynamic_update_index_in_dim(window_k, group_k, 0, 0)
    window_v = lax.dynamic_update_index_in_dim(window_v, group_v, 0, 0)

    def record(distance, key_blk, value_blk, stored):
        stored_k, stored_v, running = stored
        stored_k = lax.dynamic_update_index_in_dim(stored_k, key_blk, distance, 0)
        stored_v = lax.dynamic_update_index_in_dim(stored_v, value_blk, distance, 0)
        running = absorb(
            running, queries, grad_out, key_blk, value_blk, mask_for(distance), scaling
        )
        return (stored_k, stored_v, running)

    def forward_hop(distance, carried):
        moving = shifted(as_sent(carried[0]), "cp", 1)
        return (moving, record(distance, moving[0], moving[1], carried[1]))

    finished = lax.fori_loop(
        1, REACH + 1, forward_hop, ((group_k, group_v), (window_k, window_v, summary))
    )
    window_k, window_v, summary = finished[1]
    row_peak, row_total, carried_sum = summary
    log_total = row_peak + jnp.log(row_total)
    row_delta = carried_sum / row_total

    def contribution(distance):
        key_blk = lax.dynamic_index_in_dim(window_k, distance, 0, keepdims=False)
        value_blk = lax.dynamic_index_in_dim(window_v, distance, 0, keepdims=False)
        return gradients(
            queries, grad_out, key_blk, value_blk, mask_for(distance), log_total, row_delta, scaling
        )

    grad_query, grad_key, grad_value = contribution(0)

    def backward_hop(distance, carried):
        partial_value = shifted_2(carried[1], "cp", 1)
        more_query, more_key, more_value = contribution(distance)
        return (
            carried[0] + more_query,
            (partial_value[0] + more_key, partial_value[1] + more_value),
        )

    grad_query, partial_value = lax.fori_loop(
        1, REACH + 1, backward_hop, (grad_query, (grad_key, grad_value))
    )
    partial_value = shifted_2((partial_value[0], partial_value[1]), "cp", -REACH)
    grad_key, grad_value = (
        lax.psum_scatter(partial_value[0], "tp", scatter_dimension=1, tiled=True),
        lax.psum_scatter(partial_value[1], "tp", scatter_dimension=1, tiled=True),
    )
    return (
        grad_query.astype(jnp.bfloat16),
        grad_key.astype(jnp.bfloat16),
        grad_value.astype(jnp.bfloat16),
    )


def solution(mesh):
    placed = (
        P("cp", None, "tp", None),
        P("cp", "tp", None),
        P("cp", "tp", None),
        P("cp", None, "tp", None),
        P(),
    )
    return jax.shard_map(
        per_device,
        mesh=mesh,
        in_specs=placed,
        out_specs=(P("cp", None, "tp", None), P("cp", "tp", None), P("cp", "tp", None)),
        check_vma=False,
    )
```

profile of v0, /device:TPU:20, one launch (start us, length us, event | category | flops | bytes accessed | tf_op | source)
XLA Modules:
  0.0 264.1 jit_solution(13299432605536437906)
XLA Ops:
  7.3 1.1 convert_reduce_fusion
  10.2 5.8 %all_gather.7 = bf16[128,8,128]{2,0,1:T(8,128)(2,1)S(1)} all-gather(bf16[128,2,128]{2,0,1:T(8,128)(2,1)S(1)} %copy.49), channel_id=1, replica_groups=mesh['cp'=8,'tp'=4] {'tp'}, dimensions={1}, use_global_device_ids=true | all-gather | bytes 327680 | tf_op jit(solution)/shard_map/all_gather | solution.py:94
  15.9 5.8 %all_gather.6 = bf16[128,8,128]{2,0,1:T(8,128)(2,1)S(1)} all-gather(bf16[128,2,128]{2,0,1:T(8,128)(2,1)S(1)} %copy.48), channel_id=1, replica_groups=mesh['cp'=8,'tp'=4] {'tp'}, dimensions={1}, use_global_device_ids=true | all-gather | bytes 327680 | tf_op jit(solution)/shard_map/all_gather | solution.py:93
  21.8 1.7 copy.50
  25.2 1.0 fusion.34
  26.2 1.2 dynamic_update_slice.27
  27.4 1.2 dynamic_update_slice.28
  28.6 58.7 %while.46 = (s32[]{:T(128)}, bf16[128,8,128]{2,0,1:T(8,128)(2,1)S(1)}, bf16[128,8,128]{2,0,1:T(8,128)(2,1)}, bf16[4,128,8,128]{3,1,2,0:T(8,128)(2,1)}, bf16[4,12...) while((s32[]{:T(128)}, ...), condition=%wide.region_8.9_spmd, body=%wide.region_4.8_spmd.sunk | while | flops 274788352 | bytes 13472027 | solution.py:121
  28.6 3.4 %collective-permute-start.1 = (bf16[128,8,128]{2,0,1:T(8,128)(2,1)}, bf16[128,8,128]{2,0,1:T(8,128)(2,1)S(1)}, u32[]{:S(2)}, u32[]{:S(2)}) collective-permute-start(bf16[128,8,128]{2,0,1:T(8,128)(2,1)} %get-tuple-element.1054), channel_id=1, source_target_pairs={{0,4},{4,8},{8,12},{12,16},{16,20},{20,24},{24,28},{1,5},{5,9},{9,... | collective-permute-start | bytes 786440 | tf_op jit(solution)/shard_map/while/body/eval_jaxpr/ppermute | solution.py:19
  32.0 3.4 %collective-permute-start = (bf16[128,8,128]{2,0,1:T(8,128)(2,1)S(1)}, bf16[128,8,128]{2,0,1:T(8,128)(2,1)S(1)}, u32[]{:S(2)}, u32[]{:S(2)}) collective-permute-start(bf16[128,8,128]{2,0,1:T(8,128)(2,1)S(1)} %get-tuple-element.1053), channel_id=1, source_target_pairs={{0,4},{4,8},{8,12},{12,16},{16,20},{20,24},{24,28},{1,5},{5,9},{9,... | collective-permute-start | bytes 786440 | tf_op jit(solution)/shard_map/while/body/eval_jaxpr/ppermute | solution.py:19
  35.6 9.3 %collective-permute-done = bf16[128,8,128]{2,0,1:T(8,128)(2,1)S(1)} collective-permute-done((bf16[128,8,128]{2,0,1:T(8,128)(2,1)S(1)}, bf16[128,8,128]{2,0,1:T(8,128)(2,1)S(1)}, u32[]{:S(2)}, u32[]{:S(2)}) %collective-permute-start) | collective-permute-done | bytes 262176 | tf_op jit(solution)/shard_map/while/body/eval_jaxpr/ppermute | solution.py:19
  48.7 4.3 %collective-permute-start.1 = (bf16[128,8,128]{2,0,1:T(8,128)(2,1)}, bf16[128,8,128]{2,0,1:T(8,128)(2,1)S(1)}, u32[]{:S(2)}, u32[]{:S(2)}) collective-permute-start(bf16[128,8,128]{2,0,1:T(8,128)(2,1)} %get-tuple-element.1054), channel_id=1, source_target_pairs={{0,4},{4,8},{8,12},{12,16},{16,20},{20,24},{24,28},{1,5},{5,9},{9,... | collective-permute-start | bytes 786440 | tf_op jit(solution)/shard_map/while/body/eval_jaxpr/ppermute | solution.py:19
  53.1 2.5 collective-permute-start
  55.7 8.4 %collective-permute-done = bf16[128,8,128]{2,0,1:T(8,128)(2,1)S(1)} collective-permute-done((bf16[128,8,128]{2,0,1:T(8,128)(2,1)S(1)}, bf16[128,8,128]{2,0,1:T(8,128)(2,1)S(1)}, u32[]{:S(2)}, u32[]{:S(2)}) %collective-permute-start) | collective-permute-done | bytes 262176 | tf_op jit(solution)/shard_map/while/body/eval_jaxpr/ppermute | solution.py:19
  68.0 5.2 %collective-permute-start.1 = (bf16[128,8,128]{2,0,1:T(8,128)(2,1)}, bf16[128,8,128]{2,0,1:T(8,128)(2,1)S(1)}, u32[]{:S(2)}, u32[]{:S(2)}) collective-permute-start(bf16[128,8,128]{2,0,1:T(8,128)(2,1)} %get-tuple-element.1054), channel_id=1, source_target_pairs={{0,4},{4,8},{8,12},{12,16},{16,20},{20,24},{24,28},{1,5},{5,9},{9,... | collective-permute-start | bytes 786440 | tf_op jit(solution)/shard_map/while/body/eval_jaxpr/ppermute | solution.py:19
  73.2 1.9 collective-permute-start
  75.3 8.1 %collective-permute-done = bf16[128,8,128]{2,0,1:T(8,128)(2,1)S(1)} collective-permute-done((bf16[128,8,128]{2,0,1:T(8,128)(2,1)S(1)}, bf16[128,8,128]{2,0,1:T(8,128)(2,1)S(1)}, u32[]{:S(2)}, u32[]{:S(2)}) %collective-permute-start) | collective-permute-done | bytes 262176 | tf_op jit(solution)/shard_map/while/body/eval_jaxpr/ppermute | solution.py:19
  87.3 2.2 fusion.33
  89.5 1.4 convolution_bitcast_fusion.2
  90.9 1.7 fusion.31
  92.5 1.4 fusion.40
  93.9 1.8 multiply_bitcast_fusion
  95.7 76.6 %while.47 = (s32[]{:T(128)}, f32[128,8,4,128]{0,3,2,1:T(8,128)}, f32[128,8,128]{2,0,1:T(8,128)}, f32[128,8,128]{2,0,1:T(8,128)}, bf16[4,128,8,128]{3,1,2,0:T(8,1...) while((s32[]{:T(128)}, f32[128,8,4,128]{0,3,2,1:T(8,128)}, ...), condition=%wide.region_10.11_spmd, body=%wide.region_9.10_spmd.sunk | while | flops 676249600 | bytes 41750872 | solution.py:146
  95.7 3.4 %collective-permute-start.3 = (f32[128,8,128]{2,0,1:T(8,128)}, f32[128,8,128]{2,0,1:T(8,128)}, u32[]{:S(2)}, u32[]{:S(2)}) collective-permute-start(f32[128,8,128]{2,0,1:T(8,128)} %get-tuple-element.1106), channel_id=1, source_target_pairs={{0,4},{4,8},{8,12},{12,16},{16,20},{20,24},{24,28},{28,0},{1,5},{5... | collective-permute-start | bytes 1572872 | tf_op jit(solution)/shard_map/while/body/eval_jaxpr/ppermute | solution.py:25
  99.8 1.6 fusion.115
  102.3 9.4 %collective-permute-done.3 = f32[128,8,128]{2,0,1:T(8,128)} collective-permute-done((f32[128,8,128]{2,0,1:T(8,128)}, f32[128,8,128]{2,0,1:T(8,128)}, u32[]{:S(2)}, u32[]{:S(2)}) %collective-permute-start.3) | collective-permute-done | bytes 524320 | tf_op jit(solution)/shard_map/while/body/eval_jaxpr/ppermute | solution.py:25
  111.7 2.3 fusion.117
  114.0 5.7 %collective-permute-done.2 = f32[128,8,128]{2,0,1:T(8,128)} collective-permute-done((f32[128,8,128]{2,0,1:T(8,128)}, f32[128,8,128]{2,0,1:T(8,128)}, u32[]{:S(2)}, u32[]{:S(2)}) %collective-permute-start.2) | collective-permute-done | bytes 524320 | tf_op jit(solution)/shard_map/while/body/eval_jaxpr/ppermute | solution.py:25
  119.8 2.3 fusion.116
  122.1 3.4 %collective-permute-start.3 = (f32[128,8,128]{2,0,1:T(8,128)}, f32[128,8,128]{2,0,1:T(8,128)}, u32[]{:S(2)}, u32[]{:S(2)}) collective-permute-start(f32[128,8,128]{2,0,1:T(8,128)} %get-tuple-element.1106), channel_id=1, source_target_pairs={{0,4},{4,8},{8,12},{12,16},{16,20},{20,24},{24,28},{28,0},{1,5},{5... | collective-permute-start | bytes 1572872 | tf_op jit(solution)/shard_map/while/body/eval_jaxpr/ppermute | solution.py:25
  126.2 1.6 fusion.115
  128.7 9.4 %collective-permute-done.3 = f32[128,8,128]{2,0,1:T(8,128)} collective-permute-done((f32[128,8,128]{2,0,1:T(8,128)}, f32[128,8,128]{2,0,1:T(8,128)}, u32[]{:S(2)}, u32[]{:S(2)}) %collective-permute-start.3) | collective-permute-done | bytes 524320 | tf_op jit(solution)/shard_map/while/body/eval_jaxpr/ppermute | solution.py:25
  138.1 2.3 fusion.117
  140.4 4.9 %collective-permute-done.2 = f32[128,8,128]{2,0,1:T(8,128)} collective-permute-done((f32[128,8,128]{2,0,1:T(8,128)}, f32[128,8,128]{2,0,1:T(8,128)}, u32[]{:S(2)}, u32[]{:S(2)}) %collective-permute-start.2) | collective-permute-done | bytes 524320 | tf_op jit(solution)/shard_map/while/body/eval_jaxpr/ppermute | solution.py:25
  145.3 2.3 fusion.116
  147.6 3.4 %collective-permute-start.3 = (f32[128,8,128]{2,0,1:T(8,128)}, f32[128,8,128]{2,0,1:T(8,128)}, u32[]{:S(2)}, u32[]{:S(2)}) collective-permute-start(f32[128,8,128]{2,0,1:T(8,128)} %get-tuple-element.1106), channel_id=1, source_target_pairs={{0,4},{4,8},{8,12},{12,16},{16,20},{20,24},{24,28},{28,0},{1,5},{5... | collective-permute-start | bytes 1572872 | tf_op jit(solution)/shard_map/while/body/eval_jaxpr/ppermute | solution.py:25
  151.7 1.6 fusion.115
  154.2 9.4 %collective-permute-done.3 = f32[128,8,128]{2,0,1:T(8,128)} collective-permute-done((f32[128,8,128]{2,0,1:T(8,128)}, f32[128,8,128]{2,0,1:T(8,128)}, u32[]{:S(2)}, u32[]{:S(2)}) %collective-permute-start.3) | collective-permute-done | bytes 524320 | tf_op jit(solution)/shard_map/while/body/eval_jaxpr/ppermute | solution.py:25
  163.6 2.3 fusion.117
  165.9 4.0 %collective-permute-done.2 = f32[128,8,128]{2,0,1:T(8,128)} collective-permute-done((f32[128,8,128]{2,0,1:T(8,128)}, f32[128,8,128]{2,0,1:T(8,128)}, u32[]{:S(2)}, u32[]{:S(2)}) %collective-permute-start.2) | collective-permute-done | bytes 524320 | tf_op jit(solution)/shard_map/while/body/eval_jaxpr/ppermute | solution.py:25
  170.0 2.3 fusion.116
  172.3 2.2 collective-permute-start.5
  174.5 14.0 %collective-permute-done.5 = f32[128,8,128]{2,0,1:T(8,128)S(1)} collective-permute-done((f32[128,8,128]{2,0,1:T(8,128)}, f32[128,8,128]{2,0,1:T(8,128)S(1)}, u32[]{:S(2)}, u32[]{:S(2)}) %collective-permute-start.5) | collective-permute-done | bytes 524320 | tf_op jit(solution)/shard_map/ppermute | solution.py:25
  189.3 19.3 %collective-permute-start.4 = (f32[128,8,128]{2,0,1:T(8,128)}, f32[128,8,128]{2,0,1:T(8,128)S(1)}, u32[]{:S(2)}, u32[]{:S(2)}) collective-permute-start(f32[128,8,128]{2,0,1:T(8,128)} %get-tuple-element.675), channel_id=1, source_target_pairs={{0,20},{4,24},{8,28},{12,0},{16,4},{20,8},{24,12},{28,16},{1,21},{... | collective-permute-start | bytes 1572872 | tf_op jit(solution)/shard_map/ppermute | solution.py:25
  208.6 10.0 %collective-permute-done.4 = f32[128,8,128]{2,0,1:T(8,128)S(1)} collective-permute-done((f32[128,8,128]{2,0,1:T(8,128)}, f32[128,8,128]{2,0,1:T(8,128)S(1)}, u32[]{:S(2)}, u32[]{:S(2)}) %collective-permute-start.4) | collective-permute-done | bytes 524320 | tf_op jit(solution)/shard_map/ppermute | solution.py:25
  219.5 2.9 %copy.62 = bf16[128,8,4,128]{3,2,1,0:T(4,128)(2,1)} copy(f32[128,8,4,128]{0,3,2,1:T(8,128)} %get-tuple-element.674) | data formatting | bytes 3145728 | tf_op jit(solution)/shard_map/while | solution.py:146
  222.4 9.1 %reduce-scatter.5.cloned.1.call-done = f32[128,2,128]{2,0,1:T(8,128)} async-done(((f32[128,8,128]{2,0,1:T(8,128)}), f32[128,2,128]{2,0,1:T(8,128)}) %reduce-scatter.5.cloned.1.call-update) | async-done | bytes 131088 | tf_op jit(solution)/shard_map/reduce_scatter | solution.py:152
  233.1 22.6 %reduce-scatter.3.cloned.1.call-done = f32[128,2,128]{2,0,1:T(8,128)} async-done(((f32[128,8,128]{2,0,1:T(8,128)}), f32[128,2,128]{2,0,1:T(8,128)}) %reduce-scatter.3.cloned.1.call-update) | async-done | bytes 131088 | tf_op jit(solution)/shard_map/reduce_scatter | solution.py:151
  (103 shorter events, 25.2 us)
Async XLA Ops:
  7.2 16.3 %copy-start.3 = (bf16[128,8,4,128]{3,2,1,0:T(4,128)(2,1)S(1)}, bf16[128,8,4,128]{3,2,1,0:T(4,128)(2,1)}, u32[]{:S(2)}) copy-start(bf16[128,8,4,128]{3,2,1,0:T(4,128)(2,1)} %param.12) | copy-start | bytes 3145732
  7.2 224.3 %reduce-scatter.5.cloned.1.call-start = ((), (), s32[]{:S(2)}) async-start(), calls=%async_computation.3 | async-start | bytes 655360 | tf_op jit(solution)/shard_map/reduce_scatter | solution.py:152
  15.9 11.4 %copy-start.7 = (bf16[128,8,128]{2,0,1:T(8,128)(2,1)}, bf16[128,8,128]{2,0,1:T(8,128)(2,1)S(1)}, u32[]{:S(2)}) copy-start(bf16[128,8,128]{2,0,1:T(8,128)(2,1)S(1)} %all_gather.7) | copy-start | bytes 786436
  21.8 2.3 copy-start.5
  28.6 17.2 %collective-permute-start.1 = (bf16[128,8,128]{2,0,1:T(8,128)(2,1)}, bf16[128,8,128]{2,0,1:T(8,128)(2,1)S(1)}, u32[]{:S(2)}, u32[]{:S(2)}) collective-permute-start(bf16[128,8,128]{2,0,1:T(8,128)(2,1)} %get-tuple-element.1054), channel_id=1, source_target_pairs={{0,4},{4,8},{8,12},{12,16},{16,20},{20,24},{24,28},{1,5},{5,9},{9,... | collective-permute-start | bytes 786440 | tf_op jit(solution)/shard_map/while/body/eval_jaxpr/ppermute | solution.py:19
  32.0 12.8 %collective-permute-start = (bf16[128,8,128]{2,0,1:T(8,128)(2,1)S(1)}, bf16[128,8,128]{2,0,1:T(8,128)(2,1)S(1)}, u32[]{:S(2)}, u32[]{:S(2)}) collective-permute-start(bf16[128,8,128]{2,0,1:T(8,128)(2,1)S(1)} %get-tuple-element.1053), channel_id=1, source_target_pairs={{0,4},{4,8},{8,12},{12,16},{16,20},{20,24},{24,28},{1,5},{5,9},{9,... | collective-permute-start | bytes 786440 | tf_op jit(solution)/shard_map/while/body/eval_jaxpr/ppermute | solution.py:19
  48.7 16.4 %collective-permute-start.1 = (bf16[128,8,128]{2,0,1:T(8,128)(2,1)}, bf16[128,8,128]{2,0,1:T(8,128)(2,1)S(1)}, u32[]{:S(2)}, u32[]{:S(2)}) collective-permute-start(bf16[128,8,128]{2,0,1:T(8,128)(2,1)} %get-tuple-element.1054), channel_id=1, source_target_pairs={{0,4},{4,8},{8,12},{12,16},{16,20},{20,24},{24,28},{1,5},{5,9},{9,... | collective-permute-start | bytes 786440 | tf_op jit(solution)/shard_map/while/body/eval_jaxpr/ppermute | solution.py:19
  53.1 11.1 %collective-permute-start = (bf16[128,8,128]{2,0,1:T(8,128)(2,1)S(1)}, bf16[128,8,128]{2,0,1:T(8,128)(2,1)S(1)}, u32[]{:S(2)}, u32[]{:S(2)}) collective-permute-start(bf16[128,8,128]{2,0,1:T(8,128)(2,1)S(1)} %get-tuple-element.1053), channel_id=1, source_target_pairs={{0,4},{4,8},{8,12},{12,16},{16,20},{20,24},{24,28},{1,5},{5,9},{9,... | collective-permute-start | bytes 786440 | tf_op jit(solution)/shard_map/while/body/eval_jaxpr/ppermute | solution.py:19
  68.0 16.4 %collective-permute-start.1 = (bf16[128,8,128]{2,0,1:T(8,128)(2,1)}, bf16[128,8,128]{2,0,1:T(8,128)(2,1)S(1)}, u32[]{:S(2)}, u32[]{:S(2)}) collective-permute-start(bf16[128,8,128]{2,0,1:T(8,128)(2,1)} %get-tuple-element.1054), channel_id=1, source_target_pairs={{0,4},{4,8},{8,12},{12,16},{16,20},{20,24},{24,28},{1,5},{5,9},{9,... | collective-permute-start | bytes 786440 | tf_op jit(solution)/shard_map/while/body/eval_jaxpr/ppermute | solution.py:19
  73.2 10.2 %collective-permute-start = (bf16[128,8,128]{2,0,1:T(8,128)(2,1)S(1)}, bf16[128,8,128]{2,0,1:T(8,128)(2,1)S(1)}, u32[]{:S(2)}, u32[]{:S(2)}) collective-permute-start(bf16[128,8,128]{2,0,1:T(8,128)(2,1)S(1)} %get-tuple-element.1053), channel_id=1, source_target_pairs={{0,4},{4,8},{8,12},{12,16},{16,20},{20,24},{24,28},{1,5},{5,9},{9,... | collective-permute-start | bytes 786440 | tf_op jit(solution)/shard_map/while/body/eval_jaxpr/ppermute | solution.py:19
  87.3 2.2 copy-start.4
  90.9 1.7 copy-start.6
  92.5 1.4 copy-start.2
  95.7 16.0 %collective-permute-start.3 = (f32[128,8,128]{2,0,1:T(8,128)}, f32[128,8,128]{2,0,1:T(8,128)}, u32[]{:S(2)}, u32[]{:S(2)}) collective-permute-start(f32[128,8,128]{2,0,1:T(8,128)} %get-tuple-element.1106), channel_id=1, source_target_pairs={{0,4},{4,8},{8,12},{12,16},{16,20},{20,24},{24,28},{28,0},{1,5},{5... | collective-permute-start | bytes 1572872 | tf_op jit(solution)/shard_map/while/body/eval_jaxpr/ppermute | solution.py:25
  99.1 20.7 %collective-permute-start.2 = (f32[128,8,128]{2,0,1:T(8,128)}, f32[128,8,128]{2,0,1:T(8,128)}, u32[]{:S(2)}, u32[]{:S(2)}) collective-permute-start(f32[128,8,128]{2,0,1:T(8,128)} %get-tuple-element.1105), channel_id=1, source_target_pairs={{0,4},{4,8},{8,12},{12,16},{16,20},{20,24},{24,28},{28,0},{1,5},{5... | collective-permute-start | bytes 1572872 | tf_op jit(solution)/shard_map/while/body/eval_jaxpr/ppermute | solution.py:25
  99.8 1.7 copy-start
  102.3 11.7 %copy-start.1 = (f32[128,8,4,128]{0,3,2,1:T(8,128)}, f32[128,8,4,128]{0,3,2,1:T(8,128)S(1)}, u32[]{:S(2)}) copy-start(f32[128,8,4,128]{0,3,2,1:T(8,128)S(1)} %bitcast_add_fusion.2) | copy-start | bytes 6291460 | tf_op jit(solution)/shard_map/while
  122.1 16.0 %collective-permute-start.3 = (f32[128,8,128]{2,0,1:T(8,128)}, f32[128,8,128]{2,0,1:T(8,128)}, u32[]{:S(2)}, u32[]{:S(2)}) collective-permute-start(f32[128,8,128]{2,0,1:T(8,128)} %get-tuple-element.1106), channel_id=1, source_target_pairs={{0,4},{4,8},{8,12},{12,16},{16,20},{20,24},{24,28},{28,0},{1,5},{5... | collective-permute-start | bytes 1572872 | tf_op jit(solution)/shard_map/while/body/eval_jaxpr/ppermute | solution.py:25
  125.5 19.8 %collective-permute-start.2 = (f32[128,8,128]{2,0,1:T(8,128)}, f32[128,8,128]{2,0,1:T(8,128)}, u32[]{:S(2)}, u32[]{:S(2)}) collective-permute-start(f32[128,8,128]{2,0,1:T(8,128)} %get-tuple-element.1105), channel_id=1, source_target_pairs={{0,4},{4,8},{8,12},{12,16},{16,20},{20,24},{24,28},{28,0},{1,5},{5... | collective-permute-start | bytes 1572872 | tf_op jit(solution)/shard_map/while/body/eval_jaxpr/ppermute | solution.py:25
  126.2 1.7 copy-start
  128.7 11.7 %copy-start.1 = (f32[128,8,4,128]{0,3,2,1:T(8,128)}, f32[128,8,4,128]{0,3,2,1:T(8,128)S(1)}, u32[]{:S(2)}) copy-start(f32[128,8,4,128]{0,3,2,1:T(8,128)S(1)} %bitcast_add_fusion.2) | copy-start | bytes 6291460 | tf_op jit(solution)/shard_map/while
  147.6 16.0 %collective-permute-start.3 = (f32[128,8,128]{2,0,1:T(8,128)}, f32[128,8,128]{2,0,1:T(8,128)}, u32[]{:S(2)}, u32[]{:S(2)}) collective-permute-start(f32[128,8,128]{2,0,1:T(8,128)} %get-tuple-element.1106), channel_id=1, source_target_pairs={{0,4},{4,8},{8,12},{12,16},{16,20},{20,24},{24,28},{28,0},{1,5},{5... | collective-permute-start | bytes 1572872 | tf_op jit(solution)/shard_map/while/body/eval_jaxpr/ppermute | solution.py:25
  151.0 19.0 %collective-permute-start.2 = (f32[128,8,128]{2,0,1:T(8,128)}, f32[128,8,128]{2,0,1:T(8,128)}, u32[]{:S(2)}, u32[]{:S(2)}) collective-permute-start(f32[128,8,128]{2,0,1:T(8,128)} %get-tuple-element.1105), channel_id=1, source_target_pairs={{0,4},{4,8},{8,12},{12,16},{16,20},{20,24},{24,28},{28,0},{1,5},{5... | collective-permute-start | bytes 1572872 | tf_op jit(solution)/shard_map/while/body/eval_jaxpr/ppermute | solution.py:25
  151.7 1.7 copy-start
  154.2 11.7 %copy-start.1 = (f32[128,8,4,128]{0,3,2,1:T(8,128)}, f32[128,8,4,128]{0,3,2,1:T(8,128)S(1)}, u32[]{:S(2)}) copy-start(f32[128,8,4,128]{0,3,2,1:T(8,128)S(1)} %bitcast_add_fusion.2) | copy-start | bytes 6291460 | tf_op jit(solution)/shard_map/while
  172.3 16.2 %collective-permute-start.5 = (f32[128,8,128]{2,0,1:T(8,128)}, f32[128,8,128]{2,0,1:T(8,128)S(1)}, u32[]{:S(2)}, u32[]{:S(2)}) collective-permute-start(f32[128,8,128]{2,0,1:T(8,128)} %get-tuple-element.676), channel_id=1, source_target_pairs={{0,20},{4,24},{8,28},{12,0},{16,4},{20,8},{24,12},{28,16},{1,21},{... | collective-permute-start | bytes 1572872 | tf_op jit(solution)/shard_map/ppermute | solution.py:25
  188.4 0.8 copy-start.8
  189.3 66.4 %reduce-scatter.3.cloned.1.call-start = ((), (), s32[]{:S(2)}) async-start(), calls=%async_computation.2 | async-start | bytes 655360 | tf_op jit(solution)/shard_map/reduce_scatter | solution.py:151
  189.3 29.4 %collective-permute-start.4 = (f32[128,8,128]{2,0,1:T(8,128)}, f32[128,8,128]{2,0,1:T(8,128)S(1)}, u32[]{:S(2)}, u32[]{:S(2)}) collective-permute-start(f32[128,8,128]{2,0,1:T(8,128)} %get-tuple-element.675), channel_id=1, source_target_pairs={{0,20},{4,24},{8,28},{12,0},{16,4},{20,8},{24,12},{28,16},{1,21},{... | collective-permute-start | bytes 1572872 | tf_op jit(solution)/shard_map/ppermute | solution.py:25
  218.7 0.8 copy-start.9
Sparse Core Ops, SparseCore 0:
  189.4 42.0 reduce-scatter.4
  234.0 21.6 reduce-scatter.2
where the time goes:
time: 267 us; the launch traced here: 264 us
  waiting for transfers between devices  124 us (46%)
  starting transfers between devices  52.6 us (20%)
  matrix products  36.2 us (14%)
  local copies, waits for them, and re-layouts  19 us (7%)
  between operations  14.2 us (5%)
  blocking collectives  11.6 us (4%)
  other arithmetic  5.77 us (2%)
    ppermute x8, waiting for transfers between devices, shifted_2(): return lax.ppermute(value, axis, pairs)  66.9 us
    ppermute x8, starting transfers between devices, shifted_2(): return lax.ppermute(value, axis, pairs)  31.7 us
    ppermute x6, waiting for transfers between devices, shifted(): return lax.ppermute(block, axis, route)  25.8 us
    reduce_scatter x1, waiting for transfers between devices, per_device(): lax.psum_scatter(partial_value[0], 'tp', scatter_dimension=1, tiled=True)  22.6 us
    ppermute x6, starting transfers between devices, shifted(): return lax.ppermute(block, axis, route)  20.8 us
    reduce_scatter x1, waiting for transfers between devices, per_device(): lax.psum_scatter(partial_value[1], 'tp', scatter_dimension=1, tiled=True)  9.09 us
    dot_general x4, matrix products, gradients(): jnp.einsum('ghij,ighc->jgc', grad_logit, queries, preferred_element_type=...  8.29 us
    dot_general x4, matrix products, gradients(): jnp.einsum('ghij,ighc->jgc', weights_half, grad_out, preferred_element_ty...  8.27 us
  transfers between devices with their start and end apart: 16, of which 13 were waited for; matrix products, arithmetic and copies ran while one was open for 9% of the time, Pallas kernels for 0%

commit v1 on v0

v1 whole, which is shorter than its diff:
```python
import functools
import math

import jax
import jax.numpy as jnp
from jax import lax
from jax.experimental import pallas as pl
from jax.experimental.pallas import tpu as pltpu
from jax.sharding import PartitionSpec as P

REACH = 3
FIRST_DOC = 384
NEG = -1e30
MESH = pl.DeviceIdType.MESH
F32 = jnp.float32
BF16 = jnp.bfloat16
NT = (((1,), (1,)), ((), ()))


def dot(a, b):
    return jnp.dot(a, b, preferred_element_type=F32)


def dot_nt(a, b):
    return lax.dot_general(a, b, NT, preferred_element_type=F32)


def kernel(
    n_cp, n_tp, heads, chunk,
    q_ref, do_ref, kv_ref, starts_ref,
    dq_ref, dkv_ref,
    win, bias, p0, pb, r1, r2, r3, ts, fb,
    rs_w, rs_f, ss_1, ss_2, ss_3, ss_4, rs_1, rs_2, rs_3, sb_1, sb_2, sb_3, sb_f,
):
    me = lax.axis_index("cp")
    t = lax.axis_index("tp")
    hps, _, tok, dim = kv_ref.shape
    rows = q_ref.shape[1]
    span = (REACH + 1) * tok
    lead = FIRST_DOC // tok
    scaling = dim ** (-0.5)
    peer = (t, t + 1 - 2 * (t % 2), (t + n_tp // 2) % n_tp, n_tp - 1 - t)

    def sees(i, d):
        return (i - d >= 0) & ((i < lead) | (i - d >= lead))

    def gets(d):
        return sees(me, d)

    def gives(d):
        return (me + d < n_cp) & sees(me + d, d)

    def copy(src, dst, send, recv, where):
        return pltpu.make_async_remote_copy(
            src_ref=src, dst_ref=dst, send_sem=send, recv_sem=recv,
            device_id=where, device_id_type=MESH,
        )

    def to_cp(i):
        return {"cp": i}

    def to_tp(s):
        return {"tp": peer[s]}

    def f1(h, d):
        return copy(kv_ref.at[h], win.at[0, h, d], ss_1.at[h, d], rs_w.at[0, h, d], to_cp(me + d))

    def f_src(h, d):
        return kv_ref.at[h] if d == 0 else win.at[0, h, d]

    def f2(h, d):
        return copy(f_src(h, d), win.at[1, h, d], ss_2.at[h, d], rs_w.at[1, h, d], to_tp(1))

    def f3(h, d):
        return copy(f_src(h, d), win.at[2, h, d], ss_3.at[h, d], rs_w.at[2, h, d], to_tp(2))

    def f4(h, d):
        return copy(win.at[2, h, d], win.at[3, h, d], ss_4.at[h, d], rs_w.at[3, h, d], to_tp(1))

    def b1(h):
        return copy(pb.at[1, h], r1.at[h], sb_1.at[h], rs_1.at[h], to_tp(1))

    def b2(h):
        return copy(pb.at[2, h], r2.at[h], sb_2.at[h], rs_2.at[h], to_tp(2))

    def b3(h):
        return copy(pb.at[3, h], r3.at[h], sb_3.at[h], rs_3.at[h], to_tp(1))

    def bf(h, d):
        return copy(ts.at[h, d], fb.at[h, d], sb_f.at[h, d], rs_f.at[h, d], to_cp(me - d))

    def when_d(cond, d, action):
        if d == 0:
            action()
        else:
            pl.when(cond(d))(action)

    barrier = pltpu.get_barrier_semaphore()
    for s in (1, 2):
        pl.semaphore_signal(barrier, inc=1, device_id=to_tp(s), device_id_type=MESH)
    count = jnp.int32(2)
    for d in range(1, REACH + 1):
        count += gets(d).astype(jnp.int32) + gives(d).astype(jnp.int32)

        @pl.when(gets(d))
        def _():
            pl.semaphore_signal(barrier, inc=1, device_id=to_cp(me - d), device_id_type=MESH)

        @pl.when(gives(d))
        def _():
            pl.semaphore_signal(barrier, inc=1, device_id=to_cp(me + d), device_id_type=MESH)

    pl.semaphore_wait(barrier, count)

    for h in range(hps):
        f3(h, 0).start()
        for d in range(1, REACH + 1):
            pl.when(gives(d))(lambda: f1(h, d).start())
        f2(h, 0).start()

    for d in range(1, REACH + 1):

        @pl.when(jnp.logical_not(gets(d)))
        def _():
            for s in range(4):
                for h in range(hps):
                    win[s, h, d] = jnp.zeros(win.shape[3:], BF16)

    for h in range(hps):
        win[0, h, 0] = kv_ref[h]

    shift = heads.bit_length() - 1
    place = me * tok + lax.shift_right_logical(
        lax.broadcasted_iota(jnp.int32, (rows, 128), 0), shift
    )

    def scan(c, best):
        entry = starts_ref[pl.ds(c, 1), :]
        return jnp.maximum(best, jnp.where(entry <= place, entry, 0))

    best = lax.fori_loop(0, starts_ref.shape[0], scan, jnp.zeros((rows, 128), jnp.int32))
    start = jnp.max(jnp.transpose(best.astype(F32)), axis=0, keepdims=True).astype(jnp.int32)
    own = me * tok + lax.shift_right_logical(
        lax.broadcasted_iota(jnp.int32, (tok, rows), 1), shift
    )
    for d in range(REACH + 1):
        key = (me - d) * tok + lax.broadcasted_iota(jnp.int32, (tok, rows), 0)
        bias[d * tok:(d + 1) * tok, :] = jnp.where((key >= start) & (key <= own), 0.0, NEG)

    def compute(s, h):
        g = peer[s] * hps + h
        keys = win[s, h, :, 0].reshape(span, dim)
        values = win[s, h, :, 1].reshape(span, dim)
        keys_t = keys.T
        dk = jnp.zeros((span, dim), F32)
        dv = jnp.zeros((span, dim), F32)
        for r in range(0, rows, chunk):
            q = q_ref[g, r:r + chunk, :]
            do = do_ref[g, r:r + chunk, :]
            logits = dot_nt(keys, q) * (scaling * math.log2(math.e)) + bias[:, r:r + chunk]
            grad_prob = dot_nt(values, do)
            w = jnp.exp2(logits - jnp.max(logits, axis=0, keepdims=True))
            inv = 1.0 / jnp.sum(w, axis=0, keepdims=True)
            delta = jnp.sum(w * grad_prob, axis=0, keepdims=True) * inv
            probs = w * inv
            grad_logit = (probs * (grad_prob - delta)).astype(BF16)
            dv += dot(probs.astype(BF16), do)
            dk += dot(grad_logit, q)
            dq_t = dot(keys_t, grad_logit) * scaling
            dq_ref[g, r:r + chunk, :] = dq_t.T.astype(BF16)
        dk = (dk * scaling).reshape(REACH + 1, tok, dim)
        dv = dv.reshape(REACH + 1, tok, dim)
        if s == 0:
            p0[h, :, 0] = dk
            p0[h, :, 1] = dv
        elif s == 2:
            b3(h).wait_recv()
            pb[2, h, :, 0] = (dk + r3[h, :, 0].astype(F32)).astype(BF16)
            pb[2, h, :, 1] = (dv + r3[h, :, 1].astype(F32)).astype(BF16)
        else:
            pb[s, h, :, 0] = dk.astype(BF16)
            pb[s, h, :, 1] = dv.astype(BF16)

    def spread(h):
        for d in range(1, REACH + 1):

            @pl.when(gets(d))
            def _():
                f1(h, d).wait_recv()
                f3(h, d).start()
                f2(h, d).start()

    def relay(h):
        for d in range(REACH + 1):

            def go():
                f3(h, d).wait_recv()
                f4(h, d).start()

            when_d(gets, d, go)

    def arrived(f, h):
        for d in range(REACH + 1):
            when_d(gets, d, lambda: f(h, d).wait_recv())

    for h in range(hps):
        spread(h)
        compute(0, h)
    relay(0)
    for h in range(hps):
        arrived(f2, h)
        compute(1, h)
        b1(h).start()
        if h == 0:
            for k in range(1, hps):
                relay(k)
    for h in range(hps):
        arrived(f4, h)
        compute(3, h)
        b3(h).start()
        compute(2, h)
        b2(h).start()

    for h in range(hps):
        b1(h).wait_recv()
        b2(h).wait_recv()
        for d in range(REACH, -1, -1):
            total = p0[h, d] + r1[h, d].astype(F32) + r2[h, d].astype(F32)
            if d == 0:
                p0[h, d] = total
            else:
                ts[h, d] = total.astype(BF16)
                pl.when(gets(d))(lambda: bf(h, d).start())

    for h in range(hps):
        for d in range(1, REACH + 1):

            @pl.when(gives(d))
            def _():
                bf(h, d).wait_recv()
                p0[h, 0] += fb[h, d].astype(F32)

        dkv_ref[h] = p0[h, 0].astype(BF16)

    for h in range(hps):
        b1(h).wait_send()
        b2(h).wait_send()
        b3(h).wait_send()
        for d in range(REACH + 1):

            def sent():
                f2(h, d).wait_send()
                f3(h, d).wait_send()
                f4(h, d).wait_send()
                if d:
                    bf(h, d).wait_send()

            when_d(gets, d, sent)
            if d:
                pl.when(gives(d))(lambda: f1(h, d).wait_send())


def per_device(n_cp, n_tp, queries, key_heads, value_heads, grad_out, doc_starts):
    tok, kvh, heads, dim = queries.shape
    hps = key_heads.shape[1]
    rows = tok * heads
    reach = REACH + 1
    q = queries.transpose(1, 0, 2, 3).reshape(kvh, rows, dim)
    do = grad_out.transpose(1, 0, 2, 3).reshape(kvh, rows, dim)
    kv = jnp.stack([key_heads.transpose(1, 0, 2), value_heads.transpose(1, 0, 2)], axis=1)
    starts = doc_starts.reshape(-1, 128)
    unit = (2, tok, dim)
    dma = pltpu.SemaphoreType.DMA
    vmem = pl.BlockSpec(memory_space=pltpu.VMEM)
    dq, dkv = pl.pallas_call(
        functools.partial(kernel, n_cp, n_tp, heads, rows // 2),
        out_shape=(
            jax.ShapeDtypeStruct((kvh, rows, dim), BF16),
            jax.ShapeDtypeStruct((hps,) + unit, BF16),
        ),
        in_specs=[vmem] * 4,
        out_specs=(vmem, vmem),
        scratch_shapes=[
            pltpu.VMEM((4, hps, reach) + unit, BF16),
            pltpu.VMEM((reach * tok, rows), F32),
            pltpu.VMEM((hps, reach) + unit, F32),
            pltpu.VMEM((4, hps, reach) + unit, BF16),
            pltpu.VMEM((hps, reach) + unit, BF16),
            pltpu.VMEM((hps, reach) + unit, BF16),
            pltpu.VMEM((hps, reach) + unit, BF16),
            pltpu.VMEM((hps, reach) + unit, BF16),
            pltpu.VMEM((hps, reach) + unit, BF16),
            dma((4, hps, reach)),
            dma((hps, reach)),
            dma((hps, reach)),
            dma((hps, reach)),
            dma((hps, reach)),
            dma((hps, reach)),
            dma((hps,)),
            dma((hps,)),
            dma((hps,)),
            dma((hps,)),
            dma((hps,)),
            dma((hps,)),
            dma((hps, reach)),
        ],
        compiler_params=pltpu.CompilerParams(
            collective_id=0, has_side_effects=True, vmem_limit_bytes=56 * 1024 * 1024
        ),
    )(q, do, kv, starts)
    return (
        dq.reshape(kvh, tok, heads, dim).transpose(1, 0, 2, 3),
        dkv[:, 0].transpose(1, 0, 2),
        dkv[:, 1].transpose(1, 0, 2),
    )


def solution(mesh):
    placed = (
        P("cp", None, "tp", None),
        P("cp", "tp", None),
        P("cp", "tp", None),
        P("cp", None, "tp", None),
        P(),
    )
    return jax.shard_map(
        functools.partial(per_device, mesh.shape["cp"], mesh.shape["tp"]),
        mesh=mesh,
        in_specs=placed,
        out_specs=(P("cp", None, "tp", None), P("cp", "tp", None), P("cp", "tp", None)),
        check_vma=False,
    )
```

time: 267 us -> 53.8 us (0.20)
  waiting for transfers between devices: 124 us -> 0 us
  starting transfers between devices: 52.6 us -> 0 us
  Pallas kernels: 0 us -> 43.4 us
  matrix products: 36.2 us -> 0 us
  between operations: 14.2 us -> 0.66 us
  blocking collectives: 11.6 us -> 0 us
  local copies, waits for them, and re-layouts: 19 us -> 8.91 us
  other arithmetic: 5.77 us -> 0.67 us
    ppermute x14 -> x0, waiting for transfers between devices: 92.7 us -> none  [the longest x8 66.9 us: shifted_2(): return lax.ppermute(value, axis, pairs)]
    ppermute x14 -> x0, starting transfers between devices: 52.6 us -> none  [the longest x8 31.7 us: shifted_2(): return lax.ppermute(value, axis, pairs)]
    pallas_call x0 -> x1, Pallas kernels: none -> 43.4 us  [per_device(): pl.pallas_call(functools.partial(kernel, n_cp, n_tp, heads, rows // 2), o...]
    dot_general x28 -> x0, matrix products: 36.2 us -> none  [the longest x4 8.29 us: gradients(): jnp.einsum('ghij,ighc->jgc', grad_logit, queries, preferred_element_type=...]
    reduce_scatter x2 -> x0, waiting for transfers between devices: 31.6 us -> none  [the longest x1 22.6 us: per_device(): lax.psum_scatter(partial_value[0], 'tp', scatter_dimension=1, tiled=True)]
    all_gather x2 -> x0, blocking collectives: 11.6 us -> none  [the longest x1 5.84 us: per_device(): lax.all_gather(key_heads, 'tp', axis=1, tiled=True)]
    dynamic_update_slice x8 -> x0, local copies, waits for them, and re-layouts: 6.69 us -> none  [the longest x3 2.18 us: record(): stored_k = lax.dynamic_update_index_in_dim(stored_k, key_blk, distance, 0)]
    unnamed x22 -> x6, local copies, waits for them, and re-layouts: 6.85 us -> 1.4 us
  transfers between devices with their start and end apart: 16 -> 0, of which waited for: 13 -> 0; matrix products, arithmetic and copies ran while one was open for 9% -> 0% of each run, Pallas kernels for 0% -> 0%
where the time goes in v1:
time: 53.8 us; the launch traced here: 53.6 us
  Pallas kernels  43.4 us (81%)
  local copies, waits for them, and re-layouts  8.91 us (17%)
  other arithmetic  0.67 us (1%)
  between operations  0.66 us (1%)
    pallas_call x1, Pallas kernels, per_device(): pl.pallas_call(functools.partial(kernel, n_cp, n_tp, heads, rows // 2), o...  43.4 us
    transpose x1, local copies, waits for them, and re-layouts, per_device(): q = queries.transpose(1, 0, 2, 3).reshape(kvh, rows, dim)  2.64 us
    reshape x1, local copies, waits for them, and re-layouts, per_device(): dq.reshape(kvh, tok, heads, dim).transpose(1, 0, 2, 3)  2.59 us
    unnamed x6, local copies, waits for them, and re-layouts  1.4 us
    transpose x1, local copies, waits for them, and re-layouts, per_device(): do = grad_out.transpose(1, 0, 2, 3).reshape(kvh, rows, dim)  1.37 us

profile of v1, /device:TPU:20, one launch (start us, length us, event | category | flops | bytes accessed | tf_op | source)
XLA Modules:
  0.0 53.6 jit_solution(13573909039903625195)
XLA Ops:
  0.6 0.9 %copy_bitcast_fusion.1 = (bf16[2,1,128,128]{3,2,1,0:T(8,128)(2,1)S(1)}, bf16[2,1,128,128]{3,2,1,0:T(8,128)(2,1)S(1)}) fusion(bf16[128,2,128]{2,1,0:T(2,128)(2,1)} %param.7, bf16[128,2,128]{2,1,0:T(2,128)(2,1)} %param.6), kind=kLoop, calls=%fused_computation.2 | loop fusion | bytes 262144 | tf_op jit(solution)/shard_map/stack | solution.py:270
  1.5 0.7 %pad_maximum_fusion.kv_ref = bf16[2,2,128,128]{3,2,1,0:T(8,128)(2,1)} fusion(bf16[2,1,128,128]{3,2,1,0:T(8,128)(2,1)S(1)} %get-tuple-element.12, bf16[2,1,128,128]{3,2,1,0:T(8,128)(2,1)S(1)} %get-tuple-element.13), kind=kLoop, calls=%fused_computation.1 | loop fusion | flops 65536 | bytes 262144 | tf_op jit(solution)/shard_map/stack | solution.py:270
  2.2 0.0 copy-start
  2.2 2.6 %copy.8 = bf16[8,128,4,128]{3,2,1,0:T(4,128)(2,1)} copy(bf16[8,128,4,128]{3,2,0,1:T(4,128)(2,1)} %bitcast.27) | data formatting | bytes 2097152 | tf_op jit(solution)/shard_map/transpose | solution.py:268
  4.8 0.0 copy-done
  4.8 1.4 %copy.9 = bf16[8,128,4,128]{3,2,1,0:T(4,128)(2,1)} copy(bf16[8,128,4,128]{3,2,0,1:T(4,128)(2,1)S(1)} %bitcast.28) | data formatting | bytes 2097152 | tf_op jit(solution)/shard_map/transpose | solution.py:269
  6.2 43.4 %shard_map.76 = (bf16[8,512,128]{2,1,0:T(8,128)(2,1)}, bf16[2,2,128,128]{3,2,1,0:T(8,128)(2,1)}) custom-call(bf16[8,512,128]{2,1,0:T(8,128)(2,1)} %bitcast.25, bf16[8,512,128]{2,1,0:T(8,128)(2,1)} %bitcast.26, bf16[2,2,128,128]{3,2,1,0:T(8,128)(2,1)} %pad_maximum_fusion.kv_ref, s32[8,128]{1,0:T(8,128)} %bitcast.31), custom_call_target="tpu_custom_call" | custom-call | tf_op jit(solution)/shard_map/pallas_call | solution.py:275
  49.6 0.0 copy-start.1
  49.6 2.6 %copy.18 = bf16[8,128,4,128]{3,2,0,1:T(4,128)(2,1)} copy(bf16[8,128,4,128]{3,2,1,0:T(4,128)(2,1)} %bitcast.30) | data formatting | bytes 2097152 | tf_op jit(solution)/shard_map/reshape | solution.py:312
  52.2 0.0 copy-done.1
  52.2 0.7 %copy.14 = bf16[128,2,128]{2,1,0:T(2,128)(2,1)} copy(bf16[128,2,128]{2,0,1:T(8,128)(2,1)S(1)} %get-tuple-element.10) | data formatting | bytes 131072
  52.9 0.7 %copy.13 = bf16[128,2,128]{2,1,0:T(2,128)(2,1)} copy(bf16[128,2,128]{2,0,1:T(8,128)(2,1)S(1)} %get-tuple-element.11) | data formatting | bytes 131072
  (1 shorter events, 0.0 us)
Async XLA Ops:
  2.2 2.6 %copy-start = (bf16[128,8,4,128]{3,2,1,0:T(4,128)(2,1)S(1)}, bf16[128,8,4,128]{3,2,1,0:T(4,128)(2,1)}, u32[]{:S(2)}) copy-start(bf16[128,8,4,128]{3,2,1,0:T(4,128)(2,1)} %param.8) | copy-start | bytes 3145732
  49.6 2.6 %copy-start.1 = (bf16[2,2,128,128]{3,2,1,0:T(8,128)(2,1)S(1)}, bf16[2,2,128,128]{3,2,1,0:T(8,128)(2,1)}, u32[]{:S(2)}) copy-start(bf16[2,2,128,128]{3,2,1,0:T(8,128)(2,1)} %get-tuple-element.6) | copy-start | bytes 393220

commit v2 on v1

--- a/solution.py
+++ b/solution.py
@@ -27,15 +27,16 @@
 
 def kernel(
     n_cp, n_tp, heads, chunk,
-    q_ref, do_ref, kv_ref, starts_ref,
-    dq_ref, dkv_ref,
-    win, bias, p0, pb, r1, r2, r3, ts, fb,
+    q_hbm, do_hbm, k_ref, v_ref, starts_ref,
+    dq_hbm, dk_ref, dv_ref,
+    qs, dos, dqs, win, bias, p0, pb, r1, r2, r3, ts, fb,
     rs_w, rs_f, ss_1, ss_2, ss_3, ss_4, rs_1, rs_2, rs_3, sb_1, sb_2, sb_3, sb_f,
+    sem_q, sem_do, sem_dq,
 ):
     me = lax.axis_index("cp")
     t = lax.axis_index("tp")
-    hps, _, tok, dim = kv_ref.shape
-    rows = q_ref.shape[1]
+    tok, hps, dim = k_ref.shape
+    rows = tok * heads
     span = (REACH + 1) * tok
     lead = FIRST_DOC // tok
     scaling = dim ** (-0.5)
@@ -63,16 +64,13 @@
         return {"tp": peer[s]}
 
     def f1(h, d):
-        return copy(kv_ref.at[h], win.at[0, h, d], ss_1.at[h, d], rs_w.at[0, h, d], to_cp(me + d))
-
-    def f_src(h, d):
-        return kv_ref.at[h] if d == 0 else win.at[0, h, d]
+        return copy(win.at[0, h, 0], win.at[0, h, d], ss_1.at[h, d], rs_w.at[0, h, d], to_cp(me + d))
 
     def f2(h, d):
-        return copy(f_src(h, d), win.at[1, h, d], ss_2.at[h, d], rs_w.at[1, h, d], to_tp(1))
+        return copy(win.at[0, h, d], win.at[1, h, d], ss_2.at[h, d], rs_w.at[1, h, d], to_tp(1))
 
     def f3(h, d):
-        return copy(f_src(h, d), win.at[2, h, d], ss_3.at[h, d], rs_w.at[2, h, d], to_tp(2))
+        return copy(win.at[0, h, d], win.at[2, h, d], ss_3.at[h, d], rs_w.at[2, h, d], to_tp(2))
 
     def f4(h, d):
         return copy(win.at[2, h, d], win.at[3, h, d], ss_4.at[h, d], rs_w.at[3, h, d], to_tp(1))
@@ -80,8 +78,8 @@
     def b1(h):
         return copy(pb.at[1, h], r1.at[h], sb_1.at[h], rs_1.at[h], to_tp(1))
 
-    def b2(h):
-        return copy(pb.at[2, h], r2.at[h], sb_2.at[h], rs_2.at[h], to_tp(2))
+    def b2(h, d):
+        return copy(pb.at[2, h, d], r2.at[h, d], sb_2.at[h, d], rs_2.at[h, d], to_tp(2))
 
     def b3(h):
         return copy(pb.at[3, h], r3.at[h], sb_3.at[h], rs_3.at[h], to_tp(1))
@@ -94,6 +92,22 @@
             action()
         else:
             pl.when(cond(d))(action)
+
+    def local(array, scratch, sem, s, h):
+        return pltpu.make_async_copy(
+            array.at[:, peer[s] * hps + h], scratch.at[s, h], sem.at[s, h]
+        )
+
+    def fetch_q(s, h):
+        return local(q_hbm, qs, sem_q, s, h)
+
+    def fetch_do(s, h):
+        return local(do_hbm, dos, sem_do, s, h)
+
+    def put_dq(s, h):
+        return pltpu.make_async_copy(
+            dqs.at[s, h], dq_hbm.at[:, peer[s] * hps + h], sem_dq.at[s, h]
+        )
 
     barrier = pltpu.get_barrier_semaphore()
     for s in (1, 2):
@@ -110,6 +124,10 @@
         def _():
             pl.semaphore_signal(barrier, inc=1, device_id=to_cp(me + d), device_id_type=MESH)
 
+    for h in range(hps):
+        win[0, h, 0, 0] = k_ref[:, h, :]
+        win[0, h, 0, 1] = v_ref[:, h, :]
+
     pl.semaphore_wait(barrier, count)
 
     for h in range(hps):
@@ -126,8 +144,10 @@
                 for h in range(hps):
                     win[s, h, d] = jnp.zeros(win.shape[3:], BF16)
 
-    for h in range(hps):
-        win[0, h, 0] = kv_ref[h]
+    for s in (0, 3, 2, 1):
+        for h in range(hps):
+            fetch_q(s, h).start()
+            fetch_do(s, h).start()
 
     shift = heads.bit_length() - 1
     place = me * tok + lax.shift_right_logical(
@@ -148,15 +168,18 @@
         bias[d * tok:(d + 1) * tok, :] = jnp.where((key >= start) & (key <= own), 0.0, NEG)
 
     def compute(s, h):
-        g = peer[s] * hps + h
+        fetch_q(s, h).wait()
+        fetch_do(s, h).wait()
+        q_all = qs[s, h].reshape(rows, dim)
+        do_all = dos[s, h].reshape(rows, dim)
         keys = win[s, h, :, 0].reshape(span, dim)
         values = win[s, h, :, 1].reshape(span, dim)
         keys_t = keys.T
         dk = jnp.zeros((span, dim), F32)
         dv = jnp.zeros((span, dim), F32)
         for r in range(0, rows, chunk):
-            q = q_ref[g, r:r + chunk, :]
-            do = do_ref[g, r:r + chunk, :]
+            q = q_all[r:r + chunk]
+            do = do_all[r:r + chunk]
             logits = dot_nt(keys, q) * (scaling * math.log2(math.e)) + bias[:, r:r + chunk]
             grad_prob = dot_nt(values, do)
             w = jnp.exp2(logits - jnp.max(logits, axis=0, keepdims=True))
@@ -167,7 +190,10 @@
             dv += dot(probs.astype(BF16), do)
             dk += dot(grad_logit, q)
             dq_t = dot(keys_t, grad_logit) * scaling
-            dq_ref[g, r:r + chunk, :] = dq_t.T.astype(BF16)
+            dqs[s, h, r // heads:(r + chunk) // heads] = (
+                dq_t.T.astype(BF16).reshape(chunk // heads, heads, dim)
+            )
+        put_dq(s, h).start()
         dk = (dk * scaling).reshape(REACH + 1, tok, dim)
         dv = dv.reshape(REACH + 1, tok, dim)
         if s == 0:
@@ -203,55 +229,68 @@
         for d in range(REACH + 1):
             when_d(gets, d, lambda: f(h, d).wait_recv())
 
-    for h in range(hps):
-        spread(h)
-        compute(0, h)
-    relay(0)
-    for h in range(hps):
-        arrived(f2, h)
-        compute(1, h)
-        b1(h).start()
-        if h == 0:
-            for k in range(1, hps):
-                relay(k)
-    for h in range(hps):
+    def foreign(h):
         arrived(f4, h)
         compute(3, h)
         b3(h).start()
         compute(2, h)
-        b2(h).start()
-
-    for h in range(hps):
+        for d in range(REACH, -1, -1):
+            when_d(gets, d, lambda: b2(h, d).start())
+
+    def near(h):
+        arrived(f2, h)
+        compute(1, h)
+        b1(h).start()
+
+    def settle(h):
         b1(h).wait_recv()
-        b2(h).wait_recv()
         for d in range(REACH, -1, -1):
-            total = p0[h, d] + r1[h, d].astype(F32) + r2[h, d].astype(F32)
-            if d == 0:
-                p0[h, d] = total
-            else:
-                ts[h, d] = total.astype(BF16)
-                pl.when(gets(d))(lambda: bf(h, d).start())
-
-    for h in range(hps):
-        for d in range(1, REACH + 1):
+
+            def go():
+                b2(h, d).wait_recv()
+                total = p0[h, d] + r1[h, d].astype(F32) + r2[h, d].astype(F32)
+                if d == 0:
+                    p0[h, d] = total
+                else:
+                    ts[h, d] = total.astype(BF16)
+                    bf(h, d).start()
+
+            when_d(gets, d, go)
+
+    for h in range(hps):
+        spread(h)
+        compute(0, h)
+    for h in range(hps):
+        relay(h)
+        foreign(h)
+        if h:
+            settle(h - 1)
+        near(h)
+    settle(hps - 1)
+
+    for h in range(hps):
+        for d in range(REACH, 0, -1):
 
             @pl.when(gives(d))
             def _():
                 bf(h, d).wait_recv()
                 p0[h, 0] += fb[h, d].astype(F32)
 
-        dkv_ref[h] = p0[h, 0].astype(BF16)
+        dk_ref[:, h, :] = p0[h, 0, 0].astype(BF16)
+        dv_ref[:, h, :] = p0[h, 0, 1].astype(BF16)
 
     for h in range(hps):
         b1(h).wait_send()
-        b2(h).wait_send()
         b3(h).wait_send()
+        for s in range(4):
+            put_dq(s, h).wait()
         for d in range(REACH + 1):
 
             def sent():
                 f2(h, d).wait_send()
                 f3(h, d).wait_send()
                 f4(h, d).wait_send()
+                b2(h, d).wait_send()
                 if d:
                     bf(h, d).wait_send()
 
@@ -265,22 +304,24 @@
     hps = key_heads.shape[1]
     rows = tok * heads
     reach = REACH + 1
-    q = queries.transpose(1, 0, 2, 3).reshape(kvh, rows, dim)
-    do = grad_out.transpose(1, 0, 2, 3).reshape(kvh, rows, dim)
-    kv = jnp.stack([key_heads.transpose(1, 0, 2), value_heads.transpose(1, 0, 2)], axis=1)
     starts = doc_starts.reshape(-1, 128)
     unit = (2, tok, dim)
     dma = pltpu.SemaphoreType.DMA
     vmem = pl.BlockSpec(memory_space=pltpu.VMEM)
-    dq, dkv = pl.pallas_call(
+    hbm = pl.BlockSpec(memory_space=pl.ANY)
+    return pl.pallas_call(
         functools.partial(kernel, n_cp, n_tp, heads, rows // 2),
         out_shape=(
-            jax.ShapeDtypeStruct((kvh, rows, dim), BF16),
-            jax.ShapeDtypeStruct((hps,) + unit, BF16),
+            jax.ShapeDtypeStruct(queries.shape, BF16),
+            jax.ShapeDtypeStruct(key_heads.shape, BF16),
+            jax.ShapeDtypeStruct(value_heads.shape, BF16),
         ),
-        in_specs=[vmem] * 4,
-        out_specs=(vmem, vmem),
+        in_specs=[hbm, hbm, vmem, vmem, vmem],
+        out_specs=(hbm, vmem, vmem),
         scratch_shapes=[
+            pltpu.VMEM((4, hps, tok, heads, dim), BF16),
+            pltpu.VMEM((4, hps, tok, heads, dim), BF16),
+            pltpu.VMEM((4, hps, tok, heads, dim), BF16),
             pltpu.VMEM((4, hps, reach) + unit, BF16),
             pltpu.VMEM((reach * tok, rows), F32),
             pltpu.VMEM((hps, reach) + unit, F32),
@@ -297,22 +338,20 @@
             dma((hps, reach)),
             dma((hps, reach)),
             dma((hps,)),
+            dma((hps, reach)),
             dma((hps,)),
             dma((hps,)),
+            dma((hps, reach)),
             dma((hps,)),
-            dma((hps,)),
-            dma((hps,)),
-            dma((hps, reach)),
+            dma((hps, reach)),
+            dma((4, hps)),
+            dma((4, hps)),
+            dma((4, hps)),
         ],
         compiler_params=pltpu.CompilerParams(
             collective_id=0, has_side_effects=True, vmem_limit_bytes=56 * 1024 * 1024
         ),
-    )(q, do, kv, starts)
-    return (
-        dq.reshape(kvh, tok, heads, dim).transpose(1, 0, 2, 3),
-        dkv[:, 0].transpose(1, 0, 2),
-        dkv[:, 1].transpose(1, 0, 2),
-    )
+    )(queries, grad_out, key_heads, value_heads, starts)
 
 
 def solution(mesh):

time: 53.8 us -> 44.4 us (0.83)
  local copies, waits for them, and re-layouts: 8.91 us -> 4.08 us
  Pallas kernels: 43.4 us -> 39.2 us
  other arithmetic: 0.67 us -> 0 us
    pallas_call x1, Pallas kernels: 43.4 us -> 39.2 us  [per_device(): pl.pallas_call(functools.partial(kernel, n_cp, n_tp, heads, rows // 2), o...]
    transpose x3 -> x0, local copies, waits for them, and re-layouts: 4.02 us -> none  [the longest x1 2.64 us: per_device(): q = queries.transpose(1, 0, 2, 3).reshape(kvh, rows, dim)]
    unnamed x6 -> x7, local copies, waits for them, and re-layouts: 1.4 us -> 4.08 us
    reshape x1 -> x0, local copies, waits for them, and re-layouts: 2.59 us -> none  [per_device(): dq.reshape(kvh, tok, heads, dim).transpose(1, 0, 2, 3)]
    another operation x1 -> x0, local copies, waits for them, and re-layouts: 0.89 us -> none  [per_device(): jnp.stack([key_heads.transpose(1, 0, 2), value_heads.transpose(1, 0, 2)],...]
    another operation x1 -> x0, other arithmetic: 0.67 us -> none  [per_device(): jnp.stack([key_heads.transpose(1, 0, 2), value_heads.transpose(1, 0, 2)],...]
where the time goes in v2:
time: 44.4 us; the launch traced here: 43.9 us
  Pallas kernels  39.2 us (88%)
  local copies, waits for them, and re-layouts  4.08 us (9%)
  between operations  0.65 us (1%)
    pallas_call x1, Pallas kernels, per_device(): pl.pallas_call(functools.partial(kernel, n_cp, n_tp, heads, rows // 2), o...  39.2 us
    unnamed x7, local copies, waits for them, and re-layouts  4.08 us

profile of v2, /device:TPU:20, one launch (start us, length us, event | category | flops | bytes accessed | tf_op | source)
XLA Modules:
  0.0 43.9 jit_solution(9375134334460262714)
XLA Ops:
  0.6 39.2 %shard_map.76 = (bf16[128,8,4,128]{3,2,1,0:T(4,128)(2,1)}, bf16[128,2,128]{2,1,0:T(2,128)(2,1)}, bf16[128,2,128]{2,1,0:T(2,128)(2,1)}) custom-call(bf16[128,8,4,128]{3,2,1,0:T(4,128)(2,1)} %q_hbm.1, bf16[128,8,4,128]{3,2,1,0:T(4,128)(2,1)} %do_hbm.1, bf16[128,2,128]{2,1,0:T(2,128)(2,1)} %k_ref.1, bf16[128,2,128]{2,1,0:T(2,128)(2,1)} %v_ref.1, s32[8,128]{1,0:T(8,128)} %bitcast.1), custom_call_target="tpu_custom_call" | custom-call | tf_op jit(solution)/shard_map/pallas_call | solution.py:312
  39.8 0.0 copy-start.1
  39.8 2.6 %copy.11 = bf16[128,8,4,128]{3,2,1,0:T(4,128)(2,1)} copy(bf16[128,8,4,128]{3,2,1,0:T(4,128)(2,1)} %get-tuple-element.6) | data formatting | bytes 2097152
  42.4 0.0 copy-done.1
  42.4 0.0 copy-start
  42.4 0.6 %copy.12 = bf16[128,2,128]{2,1,0:T(2,128)(2,1)} copy(bf16[128,2,128]{2,1,0:T(2,128)(2,1)S(1)} %copy-done.1) | data formatting | bytes 131072
  43.0 0.2 copy-done
  43.3 0.6 %copy.13 = bf16[128,2,128]{2,1,0:T(2,128)(2,1)} copy(bf16[128,2,128]{2,1,0:T(2,128)(2,1)S(1)} %copy-done) | data formatting | bytes 131072
Async XLA Ops:
  39.8 2.6 %copy-start.1 = (bf16[128,2,128]{2,1,0:T(2,128)(2,1)S(1)}, bf16[128,2,128]{2,1,0:T(2,128)(2,1)}, u32[]{:S(2)}) copy-start(bf16[128,2,128]{2,1,0:T(2,128)(2,1)} %get-tuple-element.7) | copy-start | bytes 196612
  42.4 0.9 %copy-start = (bf16[128,2,128]{2,1,0:T(2,128)(2,1)S(1)}, bf16[128,2,128]{2,1,0:T(2,128)(2,1)}, u32[]{:S(2)}) copy-start(bf16[128,2,128]{2,1,0:T(2,128)(2,1)} %get-tuple-element.8) | copy-start | bytes 196612

commit v3 on v2

--- a/solution.py
+++ b/solution.py
@@ -299,6 +299,17 @@
                 pl.when(gives(d))(lambda: f1(h, d).wait_send())
 
 
+def write_out(dq_in, dk_in, dv_in, dq_out, dk_out, dv_out, sems):
+    copies = [
+        pltpu.make_async_copy(src, dst, sems.at[k])
+        for k, (src, dst) in enumerate(((dq_in, dq_out), (dk_in, dk_out), (dv_in, dv_out)))
+    ]
+    for copy in copies:
+        copy.start()
+    for copy in copies:
+        copy.wait()
+
+
 def per_device(n_cp, n_tp, queries, key_heads, value_heads, grad_out, doc_starts):
     tok, kvh, heads, dim = queries.shape
     hps = key_heads.shape[1]
@@ -309,8 +320,10 @@
     dma = pltpu.SemaphoreType.DMA
     vmem = pl.BlockSpec(memory_space=pltpu.VMEM)
     hbm = pl.BlockSpec(memory_space=pl.ANY)
-    return pl.pallas_call(
-        functools.partial(kernel, n_cp, n_tp, heads, rows // 2),
+    queries = pltpu.with_memory_space_constraint(queries, pltpu.HBM)
+    grad_out = pltpu.with_memory_space_constraint(grad_out, pltpu.HBM)
+    grads = pl.pallas_call(
+        functools.partial(kernel, n_cp, n_tp, heads, rows),
         out_shape=(
             jax.ShapeDtypeStruct(queries.shape, BF16),
             jax.ShapeDtypeStruct(key_heads.shape, BF16),
@@ -349,9 +362,17 @@
             dma((4, hps)),
         ],
         compiler_params=pltpu.CompilerParams(
-            collective_id=0, has_side_effects=True, vmem_limit_bytes=56 * 1024 * 1024
+            collective_id=0, has_side_effects=True, vmem_limit_bytes=24 * 1024 * 1024
         ),
     )(queries, grad_out, key_heads, value_heads, starts)
+    return pl.pallas_call(
+        write_out,
+        out_shape=tuple(jax.ShapeDtypeStruct(g.shape, g.dtype) for g in grads),
+        in_specs=[vmem] * 3,
+        out_specs=(hbm, hbm, hbm),
+        scratch_shapes=[dma((3,))],
+        compiler_params=pltpu.CompilerParams(vmem_limit_bytes=24 * 1024 * 1024),
+    )(*grads)
 
 
 def solution(mesh):

time: 44.4 us -> 41 us (0.923)
  local copies, waits for them, and re-layouts: 4.08 us -> 2.36 us
  Pallas kernels: 39.2 us -> 37.5 us
    unnamed x7 -> x6, local copies, waits for them, and re-layouts: 4.08 us -> 2.36 us
    pallas_call x1 -> x2, Pallas kernels: 39.2 us -> 37.5 us  [the longest x1 36.5 us: per_device(): pl.pallas_call(functools.partial(kernel, n_cp, n_tp, heads, rows), out_sh...]
where the time goes in v3:
time: 41 us; the launch traced here: 40.5 us
  Pallas kernels  37.5 us (91%)
  local copies, waits for them, and re-layouts  2.36 us (6%)
  between operations  0.65 us (2%)
    pallas_call x1, Pallas kernels, per_device(): pl.pallas_call(functools.partial(kernel, n_cp, n_tp, heads, rows), out_sh...  36.5 us
    unnamed x6, local copies, waits for them, and re-layouts  2.36 us
    pallas_call x1, Pallas kernels, per_device(): pl.pallas_call(write_out, out_shape=tuple((jax.ShapeDtypeStruct(g.shape,...  1.02 us

profile of v3, /device:TPU:20, one launch (start us, length us, event | category | flops | bytes accessed | tf_op | source)
XLA Modules:
  0.0 40.5 jit_solution(15741703633497299840)
XLA Ops:
  0.6 0.0 copy-start
  0.6 0.8 %copy-done = bf16[128,2,128]{2,1,0:T(2,128)(2,1)S(1)} copy-done((bf16[128,2,128]{2,1,0:T(2,128)(2,1)S(1)}, bf16[128,2,128]{2,1,0:T(2,128)(2,1)}, u32[]{:S(2)}) %copy-start) | copy-done | bytes 65560
  1.5 0.0 copy-start.1
  1.5 0.8 %copy-done.1 = bf16[128,2,128]{2,1,0:T(2,128)(2,1)S(1)} copy-done((bf16[128,2,128]{2,1,0:T(2,128)(2,1)S(1)}, bf16[128,2,128]{2,1,0:T(2,128)(2,1)}, u32[]{:S(2)}) %copy-start.1) | copy-done | bytes 65560
  2.3 0.0 copy-start.2
  2.3 0.7 %copy-done.2 = s32[1024]{0:T(1024)S(1)} copy-done((s32[1024]{0:T(1024)S(1)}, s32[1024]{0:T(1024)}, u32[]{:S(2)}) %copy-start.2) | copy-done | bytes 4120
  3.0 36.5 %shard_map.76 = (bf16[128,8,4,128]{3,2,1,0:T(4,128)(2,1)S(1)}, bf16[128,2,128]{2,1,0:T(2,128)(2,1)S(1)}, bf16[128,2,128]{2,1,0:T(2,128)(2,1)S(1)}) custom-call(bf16[128,8,4,128]{3,2,1,0:T(4,128)(2,1)} %q_hbm.1, bf16[128,8,4,128]{3,2,1,0:T(4,128)(2,1)} %do_hbm.1, bf16[128,2,128]{2,1,0:T(2,128)(2,1)S(1)} %copy-done, bf16[128,2,128]{2,1,0:T(2,128)(2,1)S(1)} %copy-done.1, ...), custom_call_target="tpu_custom_call" | custom-call | tf_op jit(solution)/shard_map/pallas_call | solution.py:325
  39.5 1.0 %shard_map.77 = (bf16[128,8,4,128]{3,2,1,0:T(4,128)(2,1)}, bf16[128,2,128]{2,1,0:T(2,128)(2,1)}, bf16[128,2,128]{2,1,0:T(2,128)(2,1)}) custom-call(bf16[128,8,4,128]{3,2,1,0:T(4,128)(2,1)S(1)} %get-tuple-element.6.dq_in, bf16[128,2,128]{2,1,0:T(2,128)(2,1)S(1)} %get-tuple-element.7.dk_in, bf16[128,2,128]{2,1,0:T(2,128)(2,1)S(1)} %get-tuple-element.8.dv_in), custom_call_target="tpu_custom_call" | custom-call | tf_op jit(solution)/shard_map/pallas_call | solution.py:368
Async XLA Ops:
  0.6 0.8 %copy-start = (bf16[128,2,128]{2,1,0:T(2,128)(2,1)S(1)}, bf16[128,2,128]{2,1,0:T(2,128)(2,1)}, u32[]{:S(2)}) copy-start(bf16[128,2,128]{2,1,0:T(2,128)(2,1)} %k_ref.1) | copy-start | bytes 196612
  1.5 0.8 %copy-start.1 = (bf16[128,2,128]{2,1,0:T(2,128)(2,1)S(1)}, bf16[128,2,128]{2,1,0:T(2,128)(2,1)}, u32[]{:S(2)}) copy-start(bf16[128,2,128]{2,1,0:T(2,128)(2,1)} %v_ref.1) | copy-start | bytes 196612
  2.3 0.7 %copy-start.2 = (s32[1024]{0:T(1024)S(1)}, s32[1024]{0:T(1024)}, u32[]{:S(2)}) copy-start(s32[1024]{0:T(1024)} %param.9) | copy-start | bytes 12292

commit v4 on v3

--- a/solution.py
+++ b/solution.py
@@ -27,11 +27,11 @@
 
 def kernel(
     n_cp, n_tp, heads, chunk,
-    q_hbm, do_hbm, k_ref, v_ref, starts_ref,
+    q_hbm, do_hbm, k_hbm, v_hbm, starts_hbm,
     dq_hbm, dk_ref, dv_ref,
-    qs, dos, dqs, win, bias, p0, pb, r1, r2, r3, ts, fb,
+    k_ref, v_ref, starts_ref, qs, dos, dqs, win, bias, p0, pb, r1, r2, r3, ts, fb,
     rs_w, rs_f, ss_1, ss_2, ss_3, ss_4, rs_1, rs_2, rs_3, sb_1, sb_2, sb_3, sb_f,
-    sem_q, sem_do, sem_dq,
+    sem_in, sem_q, sem_do, sem_dq,
 ):
     me = lax.axis_index("cp")
     t = lax.axis_index("tp")
@@ -109,6 +109,15 @@
             dqs.at[s, h], dq_hbm.at[:, peer[s] * hps + h], sem_dq.at[s, h]
         )
 
+    fetches = [
+        pltpu.make_async_copy(src, dst, sem_in.at[k])
+        for k, (src, dst) in enumerate(
+            ((k_hbm, k_ref), (v_hbm, v_ref), (starts_hbm, starts_ref))
+        )
+    ]
+    for fetch in fetches:
+        fetch.start()
+
     barrier = pltpu.get_barrier_semaphore()
     for s in (1, 2):
         pl.semaphore_signal(barrier, inc=1, device_id=to_tp(s), device_id_type=MESH)
@@ -124,6 +133,8 @@
         def _():
             pl.semaphore_signal(barrier, inc=1, device_id=to_cp(me + d), device_id_type=MESH)
 
+    fetches[0].wait()
+    fetches[1].wait()
     for h in range(hps):
         win[0, h, 0, 0] = k_ref[:, h, :]
         win[0, h, 0, 1] = v_ref[:, h, :]
@@ -149,6 +160,7 @@
             fetch_q(s, h).start()
             fetch_do(s, h).start()
 
+    fetches[2].wait()
     shift = heads.bit_length() - 1
     place = me * tok + lax.shift_right_logical(
         lax.broadcasted_iota(jnp.int32, (rows, 128), 0), shift
@@ -320,8 +332,10 @@
     dma = pltpu.SemaphoreType.DMA
     vmem = pl.BlockSpec(memory_space=pltpu.VMEM)
     hbm = pl.BlockSpec(memory_space=pl.ANY)
-    queries = pltpu.with_memory_space_constraint(queries, pltpu.HBM)
-    grad_out = pltpu.with_memory_space_constraint(grad_out, pltpu.HBM)
+    operands = [
+        pltpu.with_memory_space_constraint(a, pltpu.HBM)
+        for a in (queries, grad_out, key_heads, value_heads, starts)
+    ]
     grads = pl.pallas_call(
         functools.partial(kernel, n_cp, n_tp, heads, rows),
         out_shape=(
@@ -329,9 +343,12 @@
             jax.ShapeDtypeStruct(key_heads.shape, BF16),
             jax.ShapeDtypeStruct(value_heads.shape, BF16),
         ),
-        in_specs=[hbm, hbm, vmem, vmem, vmem],
+        in_specs=[hbm] * 5,
         out_specs=(hbm, vmem, vmem),
         scratch_shapes=[
+            pltpu.VMEM(key_heads.shape, BF16),
+            pltpu.VMEM(value_heads.shape, BF16),
+            pltpu.VMEM(starts.shape, jnp.int32),
             pltpu.VMEM((4, hps, tok, heads, dim), BF16),
             pltpu.VMEM((4, hps, tok, heads, dim), BF16),
             pltpu.VMEM((4, hps, tok, heads, dim), BF16),
@@ -357,6 +374,7 @@
             dma((hps, reach)),
             dma((hps,)),
             dma((hps, reach)),
+            dma((3,)),
             dma((4, hps)),
             dma((4, hps)),
             dma((4, hps)),
@@ -364,7 +382,7 @@
         compiler_params=pltpu.CompilerParams(
             collective_id=0, has_side_effects=True, vmem_limit_bytes=24 * 1024 * 1024
         ),
-    )(queries, grad_out, key_heads, value_heads, starts)
+    )(*operands)
     return pl.pallas_call(
         write_out,
         out_shape=tuple(jax.ShapeDtypeStruct(g.shape, g.dtype) for g in grads),

time: 41 us -> 38.7 us (0.944)
  local copies, waits for them, and re-layouts: 2.36 us -> 0 us
    unnamed x6 -> x0, local copies, waits for them, and re-layouts: 2.36 us -> none
where the time goes in v4:
time: 38.7 us; the launch traced here: 38.2 us
  Pallas kernels  37.6 us (97%)
  between operations  0.64 us (2%)
    pallas_call x1, Pallas kernels, per_device(): pl.pallas_call(functools.partial(kernel, n_cp, n_tp, heads, rows), out_sh...  36.6 us
    pallas_call x1, Pallas kernels, per_device(): pl.pallas_call(write_out, out_shape=tuple((jax.ShapeDtypeStruct(g.shape,...  1.02 us

profile of v4, /device:TPU:20, one launch (start us, length us, event | category | flops | bytes accessed | tf_op | source)
XLA Modules:
  0.0 38.2 jit_solution(15297006100648684717)
XLA Ops:
  0.6 36.6 %shard_map.76 = (bf16[128,8,4,128]{3,2,1,0:T(4,128)(2,1)S(1)}, bf16[128,2,128]{2,1,0:T(2,128)(2,1)S(1)}, bf16[128,2,128]{2,1,0:T(2,128)(2,1)S(1)}) custom-call(bf16[128,8,4,128]{3,2,1,0:T(4,128)(2,1)} %q_hbm.1, bf16[128,8,4,128]{3,2,1,0:T(4,128)(2,1)} %do_hbm.1, bf16[128,2,128]{2,1,0:T(2,128)(2,1)} %k_hbm.1, bf16[128,2,128]{2,1,0:T(2,128)(2,1)} %v_hbm.1, ...), custom_call_target="tpu_custom_call" | custom-call | tf_op jit(solution)/shard_map/pallas_call | solution.py:339
  37.2 1.0 %shard_map.77 = (bf16[128,8,4,128]{3,2,1,0:T(4,128)(2,1)}, bf16[128,2,128]{2,1,0:T(2,128)(2,1)}, bf16[128,2,128]{2,1,0:T(2,128)(2,1)}) custom-call(bf16[128,8,4,128]{3,2,1,0:T(4,128)(2,1)S(1)} %get-tuple-element.6.dq_in, bf16[128,2,128]{2,1,0:T(2,128)(2,1)S(1)} %get-tuple-element.7.dk_in, bf16[128,2,128]{2,1,0:T(2,128)(2,1)S(1)} %get-tuple-element.8.dv_in), custom_call_target="tpu_custom_call" | custom-call | tf_op jit(solution)/shard_map/pallas_call | solution.py:386
